TPU v7x, 256 devices: a whole 4x4x8 slice. The times are simulated.
256 devices in a mesh: tile: 4 (over y), proj: 16 (over x, z_hi, core), cuts: 4 (over z_lo).
Axes of the slice: x: 4, y: 4, z: 8 (z_hi: 2, z_lo: 4; z = z_hi * 4 + z_lo), core: 2. Of those that a mesh axis runs over, the one named last changes fastest.
Arguments:
- object_field: float32 [64, 2, 384, 2048], P(('proj', 'cuts'), None, None, 'tile'), may hold values from -5 to 5
- probe_field: float32 [2, 256, 256], replicated, may hold values from -6 to 6
- amplitudes: bfloat16 [64, 4, 6, 256, 256], P(('proj', 'cuts'), 'tile'), may hold values from 0 to 16
- pos_rows: int32 [64, 4, 6], P(('proj', 'cuts'), 'tile'), may hold values from 0 to 128
- pos_cols: int32 [64, 4, 6], P(('proj', 'cuts'), 'tile'), may hold values from 0 to 512
- counts: int32 [64, 4], P(('proj', 'cuts'), 'tile'), may hold values from 1 to 6, as said below
- admm_dual: float32 [64, 32, 2048], P(('proj', 'cuts'), None, 'tile'), may hold values from -4 to 4
- volume: float32 [32, 2048, 2048], P('cuts', ('tile', 'proj')), may hold values from -6 to 6
- proj_weights: bfloat16 [16, 2048, 2048], P(None, ('tile', 'proj')), may hold values from -0.125 to 0.125
- ray_weights: float32 [16, 2048], replicated, may hold values from -0.125 to 0.125
- angle_ids: int32 [64], replicated, may hold values from 0 to 15
Outputs:
- new_object: float32 [64, 2, 384, 2048], P(('proj', 'cuts'), None, None, 'tile')
- new_probe: float32 [2, 256, 256], replicated
- new_volume: float32 [32, 2048, 2048], P('cuts', ('tile', 'proj'))
Inputs may be any that keep to these rules, and one draw needn't show every extreme that they name: `counts`: every tile holds at least one live position and at most 6; exactly one tile of one projection holds 6, every other holds at most 3.
All inputs are finite; a program needn't handle non-finite values.
Results may differ from a plain program's by a relative error of at most 0.00095.
The roundings to bfloat16 on the way count: a program that leaves them out, or rounds other values in their place, can miss the bound.
Values may be sent and summed in bfloat16 or wider, within the bound.
A program may use at most 64 MiB of HBM per device.

v0:
```python
import math
import jax
import jax.numpy as jnp
from jax import lax
from jax.sharding import PartitionSpec as P

PB = 256
tomo_step = 1.0


def shifted(value, axis, steps):
    count = lax.axis_size(axis)
    leading, last = (max(0, -steps), min(count, count - steps))
    return lax.ppermute(value, axis, [(source, source + steps) for source in range(leading, last)])


def dft_tables(side):
    indices = jnp.arange(side, dtype=jnp.int32)
    products = indices[:, None] * indices[None, :] % side
    phase_angle = products.astype(jnp.float32) * (2.0 * math.pi / side)
    norm_factor = 1.0 / math.sqrt(side)
    return (
        (jnp.cos(phase_angle) * norm_factor).astype(jnp.bfloat16),
        (-jnp.sin(phase_angle) * norm_factor).astype(jnp.bfloat16),
    )


def matmul(left, right):
    return jnp.dot(left, right, preferred_element_type=jnp.float32)


def complex_matmul(left_real, left_imag, right_real, right_imag):
    out_real = matmul(left_real, right_real) - matmul(left_imag, right_imag)
    out_imag = matmul(left_real, right_imag) + matmul(left_imag, right_real)
    return (out_real, out_imag)


def patch_terms(patch_real, patch_imag, probe_real, probe_imag, amplitude, dft_real, dft_imag):
    wave_real = (probe_real * patch_real - probe_imag * patch_imag).astype(jnp.bfloat16)
    wave_imag = (probe_real * patch_imag + probe_imag * patch_real).astype(jnp.bfloat16)
    half_real, half_imag = complex_matmul(dft_real, dft_imag, wave_real, wave_imag)
    half_real = half_real.astype(jnp.bfloat16)
    half_imag = half_imag.astype(jnp.bfloat16)
    far_real, far_imag = complex_matmul(half_real, half_imag, dft_real, dft_imag)
    modulus = jnp.sqrt(far_real * far_real + far_imag * far_imag + 0.25)
    factor = amplitude.astype(jnp.float32) / modulus - 1.0
    diff_real = (far_real * factor).astype(jnp.bfloat16)
    diff_imag = (far_imag * factor).astype(jnp.bfloat16)
    conj_imag = -dft_imag
    back_half_real, back_half_imag = complex_matmul(dft_real, conj_imag, diff_real, diff_imag)
    back_half_real = back_half_real.astype(jnp.bfloat16)
    back_half_imag = back_half_imag.astype(jnp.bfloat16)
    back_real, back_imag = complex_matmul(back_half_real, back_half_imag, dft_real, conj_imag)
    object_real = probe_real * back_real + probe_imag * back_imag
    object_imag = probe_real * back_imag - probe_imag * back_real
    probe_grad_real = patch_real * back_real + patch_imag * back_imag
    probe_grad_imag = patch_real * back_imag - patch_imag * back_real
    energy = jnp.mean(patch_real * patch_real + patch_imag * patch_imag)
    return (
        jnp.stack([object_real, object_imag]),
        jnp.stack([probe_grad_real, probe_grad_imag]),
        energy,
    )


def tile_edges(values, offset):
    return shifted(values, "tile", offset)


def on_device(
    object_field,
    probe_field,
    amplitudes,
    pos_rows,
    pos_cols,
    counts,
    admm_dual,
    volume,
    proj_weights,
    ray_weights,
    angle_ids,
):
    half_side = PB // 2
    own_object = object_field[0]
    tile_cols = own_object.shape[2]
    from_left = tile_edges(own_object[:, :, tile_cols - half_side :], 1)
    from_right = tile_edges(own_object[:, :, :half_side], -1)
    extended = jnp.concatenate([from_left, own_object, from_right], axis=2)
    dft_real, dft_imag = dft_tables(PB)
    probe_real = probe_field[0]
    probe_imag = probe_field[1]
    zero_index = jnp.zeros((), jnp.int32)
    live_count = counts[0, 0]
    slot_total = amplitudes.shape[2]

    def slot_step(slot_index, state_tuple, weight):
        grad_sum, probe_sum, energy_sum = state_tuple
        anchor = (zero_index, pos_rows[0, 0, slot_index], pos_cols[0, 0, slot_index])
        object_patch = lax.dynamic_slice(extended, anchor, (2, PB, PB))
        object_part, probe_part, energy = patch_terms(
            object_patch[0],
            object_patch[1],
            probe_real,
            probe_imag,
            amplitudes[0, 0, slot_index],
            dft_real,
            dft_imag,
        )
        current = lax.dynamic_slice(grad_sum, anchor, (2, PB, PB))
        grad_sum = lax.dynamic_update_slice(grad_sum, current + weight * object_part, anchor)
        return (grad_sum, probe_sum + weight * probe_part, energy_sum + weight * energy)

    running = (
        jnp.zeros(extended.shape, jnp.float32),
        jnp.zeros((2, PB, PB), jnp.float32),
        jnp.zeros((), jnp.float32),
    )
    running = lax.fori_loop(
        0,
        slot_total,
        lambda slot_index, state_tuple: slot_step(
            slot_index, state_tuple, (slot_index < live_count).astype(jnp.float32)
        ),
        running,
    )
    grad_sum, probe_sum, energy_sum = running
    to_right_edge = tile_edges(grad_sum[:, :, :half_side], -1)
    to_left_edge = tile_edges(grad_sum[:, :, tile_cols + half_side :], 1)
    own_cells = grad_sum[:, :, half_side : half_side + tile_cols]
    own_cells = own_cells.at[:, :, :half_side].add(to_left_edge)
    own_cells = own_cells.at[:, :, tile_cols - half_side :].add(to_right_edge)
    probe_flat = jnp.concatenate([probe_sum.reshape(-1), jnp.broadcast_to(energy_sum, (128,))])
    probe_flat = lax.psum(probe_flat, ("tile", "proj", "cuts"))
    probe_grad = probe_flat[: probe_sum.size].reshape(probe_sum.shape)
    energy = probe_flat[probe_sum.size]
    new_probe = probe_field + probe_grad / (energy + 1e-05)
    probe_peak = jnp.max(probe_real * probe_real + probe_imag * probe_imag)
    new_object = (own_object + own_cells / (probe_peak + 1e-05))[None]
    slab_total = admm_dual.shape[1]
    first_row = (own_object.shape[1] - slab_total) // 2
    slab_values = new_object[:, 1, first_row : first_row + slab_total, :] + admm_dual
    arrived = lax.all_to_all(
        lax.all_to_all(slab_values, "proj", split_axis=2, concat_axis=0, tiled=True),
        "cuts",
        split_axis=1,
        concat_axis=0,
        tiled=True,
    )
    proj_count = lax.axis_size("proj")
    cuts_count = lax.axis_size("cuts")
    slab_dev = arrived.shape[1]
    u_share = arrived.shape[2]
    projections = proj_count * cuts_count
    arrived = arrived.reshape(cuts_count, proj_count, slab_dev, u_share).transpose(1, 0, 2, 3)
    target = (
        arrived.reshape(projections, slab_dev, u_share)
        .transpose(2, 0, 1)
        .reshape(u_share, projections * slab_dev)
    )
    angle_count = ray_weights.shape[0]
    x_share = volume.shape[1]
    width = volume.shape[2]
    onehot = (angle_ids[:, None] == jnp.arange(angle_count, dtype=jnp.int32)[None, :]).astype(
        jnp.float32
    )
    ray_table = jnp.dot(
        onehot, ray_weights, precision=lax.Precision.HIGHEST, preferred_element_type=jnp.float32
    )
    ray_sums = jnp.einsum("zxy,ay->azx", volume, ray_table, precision=lax.Precision.HIGHEST).astype(
        jnp.bfloat16
    )
    spread = onehot.astype(jnp.bfloat16)[:, :, None, None] * ray_sums[:, None, :, :]
    spread = spread.transpose(1, 3, 0, 2).reshape(angle_count * x_share, projections * slab_dev)
    weight_flat = proj_weights.reshape(angle_count * x_share, width)
    partial_term = lax.dot_general(
        weight_flat, spread, (((0,), (0,)), ((), ())), preferred_element_type=jnp.float32
    )
    own_rows = lax.psum_scatter(partial_term, ("tile", "proj"), scatter_dimension=0, tiled=True)
    own_residue = (own_rows - target).astype(jnp.bfloat16)
    residue = lax.all_gather(own_residue, ("tile", "proj"), axis=0, tiled=True)
    backproj = matmul(weight_flat, residue)
    backproj = backproj.reshape(angle_count, x_share, projections, slab_dev)
    back_sums = jnp.einsum("gxaz,ag->azx", backproj, onehot, precision=lax.Precision.HIGHEST)
    gradient = jnp.einsum("azx,ay->zxy", back_sums, ray_table, precision=lax.Precision.HIGHEST)
    new_volume = volume - tomo_step * gradient
    return (new_object, new_probe, new_volume)


def solution(mesh):
    in_specs = (
        P(("proj", "cuts"), None, None, "tile"),
        P(),
        P(("proj", "cuts"), "tile", None, None, None),
        P(("proj", "cuts"), "tile", None),
        P(("proj", "cuts"), "tile", None),
        P(("proj", "cuts"), "tile"),
        P(("proj", "cuts"), None, "tile"),
        P("cuts", ("tile", "proj"), None),
        P(None, ("tile", "proj"), None),
        P(),
        P(),
    )
    out_specs = (P(("proj", "cuts"), None, None, "tile"), P(), P("cuts", ("tile", "proj"), None))
    return jax.shard_map(
        on_device, mesh=mesh, in_specs=in_specs, out_specs=out_specs, check_vma=False
    )
```

profile of v0, /device:TPU:1, one launch (start us, length us, event | category | flops | bytes accessed | tf_op | source)
XLA Modules:
  0.0 628.5 jit_solution(16933225154168796481)
XLA Ops:
  8.1 3.2 copy.17
  11.2 2.3 fusion.131
  13.5 4.0 collective-permute-start
  20.2 1.8 fusion.122
  22.1 1.6 broadcast_multiply_fusion
  23.7 3.4 mul.431
  27.1 3.3 convolution_bitcast_fusion
  30.4 5.3 copy.31
  37.5 3.2 pad_maximum_fusion
  40.7 1.6 broadcast_in_dim.6.clone
  42.3 245.5 %while.23 = (s32[]{:T(128)}, f32[2,384,768]{1,2,0:T(8,128)}, f32[2,256,256]{2,1,0:T(8,128)}, f32[]{:T(128)}, s32[1,1,6]{2,1,0:T(1,128)S(1)}, /*index=5*/s32[1,1,...) while((s32[]{:T(128)}, f32[2,384,768]{1,2,0:T(8,128)}, ...), condition=%wide.region_2.3_spmd.clone.clone, body=%wide.region_0.2_spmd.clone.clone.sunk | while | flops 558956544 | bytes 21102956 | solution.py:118
  48.1 1.7 fusion.215
  57.8 2.1 multiply_convert_fusion.39
  68.0 3.0 fusion.228
  72.5 1.3 constant_dynamic-slice_fusion.8
  75.4 6.6 %dynamic_update_slice.13 = f32[2,384,768]{1,2,0:T(8,128)} dynamic-update-slice(f32[2,384,768]{1,2,0:T(8,128)} %get-tuple-element.644, f32[2,256,256]{1,2,0:T(8,128)S(1)} %copy.50, s32[]{:T(128)} %constant.167.clone.1..sunk, s32[]{:T(128)S(6)} %select_n.153, s32[]{:T(128)S(6)} %select_n.154) | dynamic-update-slice | bytes 1048580 | tf_op jit(solution)/shard_map/while/body/eval_jaxpr/dynamic_update_slice | solution.py:110
  88.4 1.7 fusion.215
  98.1 2.1 multiply_convert_fusion.39
  108.2 3.0 fusion.228
  111.9 1.9 fusion.230
  113.8 1.3 constant_dynamic-slice_fusion.8
  116.7 6.0 dynamic_update_slice.13
  129.1 1.7 fusion.215
  138.8 2.1 multiply_convert_fusion.39
  148.9 3.0 fusion.228
  152.6 1.9 fusion.230
  154.5 1.3 constant_dynamic-slice_fusion.8
  157.4 6.2 dynamic_update_slice.13
  168.4 1.3 constant_dynamic-slice_fusion.9
  170.0 1.7 fusion.215
  179.7 2.1 multiply_convert_fusion.39
  189.9 3.0 fusion.228
  193.5 1.9 fusion.230
  195.4 1.3 constant_dynamic-slice_fusion.8
  198.3 6.3 dynamic_update_slice.13
  211.0 1.7 fusion.215
  220.7 2.1 multiply_convert_fusion.39
  230.9 3.0 fusion.228
  234.5 1.9 fusion.230
  236.5 1.3 constant_dynamic-slice_fusion.8
  239.3 6.6 %dynamic_update_slice.13 = f32[2,384,768]{1,2,0:T(8,128)} dynamic-update-slice(f32[2,384,768]{1,2,0:T(8,128)} %get-tuple-element.644, f32[2,256,256]{1,2,0:T(8,128)S(1)} %copy.50, s32[]{:T(128)} %constant.167.clone.1..sunk, s32[]{:T(128)S(6)} %select_n.153, s32[]{:T(128)S(6)} %select_n.154) | dynamic-update-slice | bytes 1048580 | tf_op jit(solution)/shard_map/while/body/eval_jaxpr/dynamic_update_slice | solution.py:110
  252.4 1.7 fusion.215
  262.0 2.1 multiply_convert_fusion.39
  272.2 3.0 fusion.228
  275.8 1.9 fusion.230
  277.7 1.3 constant_dynamic-slice_fusion.8
  280.6 6.3 %dynamic_update_slice.13 = f32[2,384,768]{1,2,0:T(8,128)} dynamic-update-slice(f32[2,384,768]{1,2,0:T(8,128)} %get-tuple-element.644, f32[2,256,256]{1,2,0:T(8,128)S(1)} %copy.50, s32[]{:T(128)} %constant.167.clone.1..sunk, s32[]{:T(128)S(6)} %select_n.153, s32[]{:T(128)S(6)} %select_n.154) | dynamic-update-slice | bytes 1048580 | tf_op jit(solution)/shard_map/while/body/eval_jaxpr/dynamic_update_slice | solution.py:110
  287.7 2.0 fusion.130
  289.7 5.9 collective-permute-start.2
  298.5 1.6 slice.103
  300.1 2.7 collective-permute-done.2
  303.9 3.2 collective-permute-done.3
  311.2 2.2 reduce.4
  313.5 22.6 %all_to_all.27 = f32[16,1,1024]{2,1,0:T(1,128)S(1)} all-to-all(f32[16,1,1024]{2,1,0:T(1,128)S(1)} %reshape.139), channel_id=1, replica_groups=mesh['tile'=4,'proj'=16,'cuts'=4] {'proj'}, dimensions={0} | all-to-all | bytes 131072 | tf_op jit(solution)/shard_map/all_to_all | solution.py:143
  340.0 3.3 all-to-all-start.1
  344.5 3.3 all-to-all-done.1
  348.8 102.0 %reduce-scatter.4.cloned.1.call-done = f32[32,512]{1,0:T(8,128)} async-done(((f32[2048,512]{1,0:T(8,128)}), f32[32,512]{1,0:T(8,128)}) %reduce-scatter.4.cloned.1.call-update) | async-done | bytes 65552
  452.6 145.6 %all-reduce.3.cloned.1.call-done = f32[131200]{0:T(1024)} async-done(((f32[131200]{0:T(1024)}), f32[131200]{0:T(1024)}) %all-reduce.3.cloned.1.call-update) | async-done | bytes 524816 | tf_op jit(solution)/shard_map/psum | solution.py:133
  600.0 1.9 slice_divide_fusion
  604.0 3.0 copy.28
  607.0 2.9 convolution_bitcast_fusion.2
  609.9 2.5 reshape.131
  612.4 3.8 fusion.126
  616.4 4.7 convolution_subtract_fusion.4
  (197 shorter events, 140.6 us)
Async XLA Ops:
  8.0 19.1 %copy-start = (bf16[16,32,2048]{2,1,0:T(8,128)(2,1)S(1)}, bf16[16,32,2048]{2,1,0:T(8,128)(2,1)}, u32[]{:S(2)}) copy-start(bf16[16,32,2048]{2,1,0:T(8,128)(2,1)} %param.25) | copy-start | bytes 6291460
  8.0 10.8 %copy-start.13 = (s32[64]{0:T(128)S(1)}, s32[64]{0:T(128)}, u32[]{:S(2)}) copy-start(s32[64]{0:T(128)} %param.27) | copy-start | bytes 772
  8.0 10.9 %copy-start.9 = (f32[16,2048]{1,0:T(8,128)S(1)}, f32[16,2048]{1,0:T(8,128)}, u32[]{:S(2)}) copy-start(f32[16,2048]{1,0:T(8,128)} %param.26) | copy-start | bytes 393220
  8.0 442.8 %reduce-scatter.4.cloned.1.call-start = ((), (), s32[]{:S(2)}) async-start(), calls=%async_computation.5 | async-start | bytes 4259840
  11.2 8.9 %copy-start.3 = (f32[8,32,2048]{2,1,0:T(8,128)S(1)}, f32[8,32,2048]{2,1,0:T(8,128)}, u32[]{:S(2)}) copy-start(f32[8,32,2048]{2,1,0:T(8,128)} %param.24) | copy-start | bytes 6291460
  13.5 24.0 %collective-permute-start = (f32[2,384,128]{1,2,0:T(8,128)}, f32[2,384,128]{1,2,0:T(8,128)S(1)}, u32[]{:S(2)}, u32[]{:S(2)}) collective-permute-start(f32[2,384,128]{1,2,0:T(8,128)} %get-tuple-element.528), channel_id=1, source_target_pairs={{0,64},{64,128},{128,192},{1,65},{65,129},{129,193},{2,66},{66,130... | collective-permute-start | bytes 1179656 | tf_op jit(solution)/shard_map/ppermute | solution.py:14
  17.6 19.9 %collective-permute-start.1 = (f32[2,384,128]{1,2,0:T(8,128)}, f32[2,384,128]{1,2,0:T(8,128)}, u32[]{:S(2)}, u32[]{:S(2)}) collective-permute-start(f32[2,384,128]{1,2,0:T(8,128)} %get-tuple-element.529), channel_id=1, source_target_pairs={{64,0},{128,64},{192,128},{65,1},{129,65},{193,129},{66,2},{130,66... | collective-permute-start | bytes 1179656 | tf_op jit(solution)/shard_map/ppermute | solution.py:14
  19.4 0.8 copy-start.7
  35.7 1.0 copy-start.5
  40.7 1.6 copy-start.11
  40.7 1.6 copy-start.12
  42.2 254.7 %copy-start.10 = (f32[1,32,512]{2,1,0:T(8,128)S(1)}, f32[1,32,512]{2,1,0:T(8,128)}, u32[]{:S(2)}) copy-start(f32[1,32,512]{2,1,0:T(8,128)} %param.23) | copy-start | bytes 196612
  287.7 9.4 %copy-start.6 = (f32[2,256,256]{2,1,0:T(8,128)S(1)}, f32[2,256,256]{2,1,0:T(8,128)}, u32[]{:S(2)}) copy-start(f32[2,256,256]{2,1,0:T(8,128)} %param.18) | copy-start | bytes 1572868
  289.7 13.1 %collective-permute-start.2 = (f32[2,384,128]{1,2,0:T(8,128)}, f32[2,384,128]{1,2,0:T(8,128)}, u32[]{:S(2)}, u32[]{:S(2)}) collective-permute-start(f32[2,384,128]{1,2,0:T(8,128)} %get-tuple-element.527), channel_id=1, source_target_pairs={{0,64},{64,128},{128,192},{1,65},{65,129},{129,193},{2,66},{66,130... | collective-permute-start | bytes 1179656 | tf_op jit(solution)/shard_map/ppermute | solution.py:14
  295.7 11.4 %collective-permute-start.3 = (f32[2,384,128]{1,2,0:T(8,128)S(1)}, f32[2,384,128]{1,2,0:T(8,128)}, u32[]{:S(2)}, u32[]{:S(2)}) collective-permute-start(f32[2,384,128]{1,2,0:T(8,128)S(1)} %get-tuple-element.526), channel_id=1, source_target_pairs={{64,0},{128,64},{192,128},{65,1},{129,65},{193,129},{66,2},{130,66... | collective-permute-start | bytes 1179656 | tf_op jit(solution)/shard_map/ppermute | solution.py:14
  298.4 9.8 %copy-start.1 = (f32[1,2,384,512]{2,3,1,0:T(8,128)S(1)}, f32[1,2,384,512]{2,3,1,0:T(8,128)}, u32[]{:S(2)}) copy-start(f32[1,2,384,512]{2,3,1,0:T(8,128)} %copy.17) | copy-start | bytes 4718596
  308.4 1.1 copy-start.4
  309.5 33.8 %copy-start.2 = (f32[2,256,256]{2,1,0:T(8,128)S(1)}, f32[2,256,256]{2,1,0:T(8,128)}, u32[]{:S(2)}) copy-start(f32[2,256,256]{2,1,0:T(8,128)} %get-tuple-element.383) | copy-start | bytes 1572868
  340.0 7.9 %all-to-all-start.1 = ((f32[4,1,4096]{2,1,0:T(1,128)}), f32[4,1,4096]{2,1,0:T(1,128)S(1)}, u32[]{:S(2)}, u32[]{:S(2)}) async-start(f32[4,1,4096]{2,1,0:T(1,128)} %reshape.141), calls=%async_computation.1 | async-start | bytes 131072 | tf_op jit(solution)/shard_map/all_to_all | solution.py:142
  343.3 254.9 %all-reduce.3.cloned.1.call-start = ((), (), s32[]{:S(2)}) async-start(), calls=%async_computation.3 | async-start | bytes 1056768 | tf_op jit(solution)/shard_map/psum | solution.py:133
  344.5 262.5 %all-gather.2.cloned.1.call-start = ((), (), s32[]{:S(2)}) async-start(), calls=%async_computation.4 | async-start | bytes 2129920 | tf_op jit(solution)/shard_map/all_gather | solution.py:180
  612.4 4.0 copy-start.8
Sparse Core Ops, SparseCore 0:
  35.8 414.9 reduce-scatter.3
  454.3 86.0 all-gather.1
Sparse Core Ops, SparseCore 1:
  349.8 248.3 all-reduce.2
where the time goes:
time: 632 us; the launch traced here: 629 us
  waiting for transfers between devices  257 us (41%)
  matrix products  143 us (23%)
  local copies, waits for them, and re-layouts  99.8 us (16%)
  other arithmetic  42.6 us (7%)
  loops' own time  30.5 us (5%)
  blocking collectives  22.6 us (4%)
  between operations  17.1 us (3%)
  starting transfers between devices  16 us (3%)
    psum x1, waiting for transfers between devices, on_device(): probe_flat = lax.psum(probe_flat, ('tile', 'proj', 'cuts'))  146 us
    dot_general x97, matrix products, matmul(): return jnp.dot(left, right, preferred_element_type=jnp.float32)  129 us
    unnamed x4, waiting for transfers between devices  102 us
    dynamic_update_slice x12, local copies, waits for them, and re-layouts, slot_step(): lax.dynamic_update_slice(grad_sum, current + weight * object_part, anchor)  39.1 us
    another operation x1, loops' own time, on_device(): lax.fori_loop(0, slot_total, lambda slot_index, state_tuple: slot_step(sl...  30.5 us
    all_to_all x1, blocking collectives, on_device(): lax.all_to_all(slab_values, 'proj', split_axis=2, concat_axis=0, tiled=True)  22.6 us
    unnamed x40, local copies, waits for them, and re-layouts  18.8 us
  transfers between devices with their start and end apart: 8, of which 5 were waited for; matrix products, arithmetic and copies ran while one was open for 42% of the time, Pallas kernels for 0%

commit v1 on v0

--- a/solution.py
+++ b/solution.py
@@ -3,6 +3,7 @@
 import jax.numpy as jnp
 from jax import lax
 from jax.sharding import PartitionSpec as P
+from jax.lax import psum
 
 PB = 256
 tomo_step = 1.0
@@ -130,7 +131,8 @@
     own_cells = own_cells.at[:, :, :half_side].add(to_left_edge)
     own_cells = own_cells.at[:, :, tile_cols - half_side :].add(to_right_edge)
     probe_flat = jnp.concatenate([probe_sum.reshape(-1), jnp.broadcast_to(energy_sum, (128,))])
-    probe_flat = lax.psum(probe_flat, ("tile", "proj", "cuts"))
+    build_sides = lambda block_in: psum(psum(block_in, ("proj", "cuts")), "tile")
+    probe_flat = build_sides(probe_flat)
     probe_grad = probe_flat[: probe_sum.size].reshape(probe_sum.shape)
     energy = probe_flat[probe_sum.size]
     new_probe = probe_field + probe_grad / (energy + 1e-05)

time: 632 us -> 823 us (1.30)
  waiting for transfers between devices: 257 us -> 446 us
  starting transfers between devices: 16 us -> 25.9 us
  blocking collectives: 22.6 us -> 13.7 us
    unnamed x4 -> x5, waiting for transfers between devices: 102 us -> 219 us
    all_gather x1, waiting for transfers between devices: 0.01 us -> 78 us  [on_device(): residue = lax.all_gather(own_residue, ('tile', 'proj'), axis=0, tiled=True)]
    all_to_all x1, starting transfers between devices: 3.28 us -> 13 us  [on_device(): lax.all_to_all(slab_values, 'proj', split_axis=2, concat_axis=0, tiled=True)]
    all_to_all x1, blocking collectives: 22.6 us -> 13.7 us  [on_device(): lax.all_to_all(lax.all_to_all(slab_values, 'proj', split_axis=2, concat_a...]
    psum x1 -> x2, waiting for transfers between devices: 146 us -> 143 us  [the longest x1 143 us: on_device(): psum(block_in, ('proj', 'cuts'))]
    unnamed x40 -> x38, local copies, waits for them, and re-layouts: 18.8 us -> 18.1 us
  transfers between devices with their start and end apart: 8 -> 9, of which waited for: 5 -> 5; matrix products, arithmetic and copies ran while one was open for 42% -> 5% of each run, Pallas kernels for 0% -> 0%
where the time goes in v1:
time: 823 us; the launch traced here: 820 us
  waiting for transfers between devices  446 us (54%)
  matrix products  145 us (18%)
  local copies, waits for them, and re-layouts  99.1 us (12%)
  other arithmetic  40.9 us (5%)
  loops' own time  32.5 us (4%)
  starting transfers between devices  25.9 us (3%)
  between operations  17.1 us (2%)
  blocking collectives  13.7 us (2%)
    unnamed x5, waiting for transfers between devices  219 us
    psum x1, waiting for transfers between devices, on_device(): psum(block_in, ('proj', 'cuts'))  143 us
    dot_general x97, matrix products, matmul(): return jnp.dot(left, right, preferred_element_type=jnp.float32)  129 us
    all_gather x1, waiting for transfers between devices, on_device(): residue = lax.all_gather(own_residue, ('tile', 'proj'), axis=0, tiled=True)  78 us
    dynamic_update_slice x12, local copies, waits for them, and re-layouts, slot_step(): lax.dynamic_update_slice(grad_sum, current + weight * object_part, anchor)  39 us
    another operation x1, loops' own time, on_device(): lax.fori_loop(0, slot_total, lambda slot_index, state_tuple: slot_step(sl...  32.5 us
    unnamed x38, local copies, waits for them, and re-layouts  18.1 us
  transfers between devices with their start and end apart: 9, of which 5 were waited for; matrix products, arithmetic and copies ran while one was open for 5% of the time, Pallas kernels for 0%

profile of v1, /device:TPU:1, one launch (start us, length us, event | category | flops | bytes accessed | tf_op | source)
XLA Modules:
  0.0 819.8 jit_solution(4945872668138544984)
XLA Ops:
  8.1 3.2 copy.17
  11.2 2.1 fusion.131
  13.3 4.0 collective-permute-start
  20.0 3.4 fusion.122
  23.5 1.6 broadcast_multiply_fusion
  25.1 4.1 mul.431
  29.9 3.1 pad_maximum_fusion
  33.1 1.6 broadcast_in_dim.6.clone
  34.7 247.7 %while.23 = (s32[]{:T(128)}, f32[2,384,768]{1,2,0:T(8,128)}, f32[2,256,256]{2,1,0:T(8,128)}, f32[]{:T(128)}, s32[1,1,6]{2,1,0:T(1,128)S(1)}, /*index=5*/s32[1,1,...) while((s32[]{:T(128)}, f32[2,384,768]{1,2,0:T(8,128)}, ...), condition=%wide.region_2.3_spmd.clone.clone, body=%wide.region_0.2_spmd.clone.clone.sunk | while | flops 558956544 | bytes 21102956 | solution.py:119
  39.3 1.3 constant_dynamic-slice_fusion.9
  40.9 1.7 fusion.215
  50.6 2.1 multiply_convert_fusion.39
  60.8 3.0 fusion.228
  65.3 1.3 constant_dynamic-slice_fusion.8
  68.2 6.5 dynamic_update_slice.13
  81.6 1.7 fusion.215
  91.3 2.1 multiply_convert_fusion.39
  101.4 3.0 fusion.228
  105.0 1.9 fusion.230
  107.0 1.3 constant_dynamic-slice_fusion.8
  109.8 6.0 dynamic_update_slice.13
  122.6 1.7 fusion.215
  132.3 2.1 multiply_convert_fusion.39
  142.5 3.0 fusion.228
  146.1 1.9 fusion.230
  148.0 1.3 constant_dynamic-slice_fusion.8
  150.9 6.2 dynamic_update_slice.13
  164.0 1.7 fusion.215
  173.7 2.1 multiply_convert_fusion.39
  183.8 3.0 fusion.228
  187.5 1.9 fusion.230
  189.4 1.3 constant_dynamic-slice_fusion.8
  192.2 6.3 dynamic_update_slice.13
  205.4 1.7 fusion.215
  215.0 2.1 multiply_convert_fusion.39
  225.2 3.0 fusion.228
  228.8 1.9 fusion.230
  230.8 1.3 constant_dynamic-slice_fusion.8
  233.6 6.5 dynamic_update_slice.13
  247.0 1.7 fusion.215
  256.7 2.1 multiply_convert_fusion.39
  266.8 3.0 fusion.228
  270.5 1.9 fusion.230
  272.4 1.3 constant_dynamic-slice_fusion.8
  275.3 6.3 dynamic_update_slice.13
  282.5 1.4 copy.40
  284.8 3.2 convolution_bitcast_fusion
  288.0 5.4 copy.31
  293.4 2.0 fusion.130
  295.4 6.1 collective-permute-start.2
  304.2 1.6 slice.103
  305.9 2.7 collective-permute-done.2
  309.7 3.2 collective-permute-done.3
  318.4 13.0 %all-to-all-start = ((f32[16,1,1024]{2,1,0:T(1,128)}), f32[16,1,1024]{2,1,0:T(1,128)S(1)}, u32[]{:S(2)}, u32[]{:S(2)}) async-start(f32[16,1,1024]{2,1,0:T(1,128)} %reshape.139), calls=%async_computation | async-start | bytes 131072 | tf_op jit(solution)/shard_map/all_to_all | solution.py:145
  331.4 142.9 %all-reduce.4.cloned.1.call-done = f32[131200]{0:T(1024)} async-done(((f32[131200]{0:T(1024)}), f32[131200]{0:T(1024)}) %all-reduce.4.cloned.1.call-update) | async-done | bytes 524816 | tf_op jit(solution)/shard_map/psum | solution.py:134
  476.0 13.7 %all_to_all.27 = f32[4,1,4096]{2,1,0:T(1,128)S(1)} all-to-all(f32[4,1,4096]{2,1,0:T(1,128)S(1)} %reshape.141), channel_id=1, replica_groups=mesh['tile'=4,'proj'=16,'cuts'=4] {'cuts'}, dimensions={0} | all-to-all | bytes 131072 | tf_op jit(solution)/shard_map/all_to_all | solution.py:144
  490.7 219.0 %reduce-scatter.4.cloned.1.call-done = f32[32,512]{1,0:T(8,128)} async-done(((f32[2048,512]{1,0:T(8,128)}), f32[32,512]{1,0:T(8,128)}) %reduce-scatter.4.cloned.1.call-update) | async-done | bytes 65552
  711.5 3.0 copy.28
  716.4 1.9 slice_divide_fusion
  720.3 78.0 %all-gather.2.cloned.1.call-done = bf16[2048,512]{1,0:T(8,128)(2,1)} async-done(((bf16[32,512]{1,0:T(8,128)(2,1)}), bf16[2048,512]{1,0:T(8,128)(2,1)}) %all-gather.2.cloned.1.call-update) | async-done | bytes 2097168 | tf_op jit(solution)/shard_map/all_gather | solution.py:182
  798.3 2.9 convolution_bitcast_fusion.2
  801.2 2.5 reshape.131
  803.7 3.8 fusion.126
  807.7 4.7 convolution_subtract_fusion.4
  (198 shorter events, 138.6 us)
Async XLA Ops:
  8.0 276.7 %copy-start = (bf16[16,32,2048]{2,1,0:T(8,128)(2,1)S(1)}, bf16[16,32,2048]{2,1,0:T(8,128)(2,1)}, u32[]{:S(2)}) copy-start(bf16[16,32,2048]{2,1,0:T(8,128)(2,1)} %param.25) | copy-start | bytes 6291460
  8.0 10.7 %copy-start.12 = (s32[64]{0:T(128)S(1)}, s32[64]{0:T(128)}, u32[]{:S(2)}) copy-start(s32[64]{0:T(128)} %param.27) | copy-start | bytes 772
  8.0 10.7 %copy-start.8 = (f32[16,2048]{1,0:T(8,128)S(1)}, f32[16,2048]{1,0:T(8,128)}, u32[]{:S(2)}) copy-start(f32[16,2048]{1,0:T(8,128)} %param.26) | copy-start | bytes 393220
  8.0 466.3 %all-reduce.4.cloned.1.call-start = ((), (), s32[]{:S(2)}) async-start(), calls=%async_computation.3 | async-start | bytes 1056768 | tf_op jit(solution)/shard_map/psum | solution.py:134
  13.3 16.6 %collective-permute-start = (f32[2,384,128]{1,2,0:T(8,128)}, f32[2,384,128]{1,2,0:T(8,128)S(1)}, u32[]{:S(2)}, u32[]{:S(2)}) collective-permute-start(f32[2,384,128]{1,2,0:T(8,128)} %get-tuple-element.528), channel_id=1, source_target_pairs={{0,64},{64,128},{128,192},{1,65},{65,129},{129,193},{2,66},{66,130... | collective-permute-start | bytes 1179656 | tf_op jit(solution)/shard_map/ppermute | solution.py:15
  17.4 12.6 %collective-permute-start.1 = (f32[2,384,128]{1,2,0:T(8,128)}, f32[2,384,128]{1,2,0:T(8,128)}, u32[]{:S(2)}, u32[]{:S(2)}) collective-permute-start(f32[2,384,128]{1,2,0:T(8,128)} %get-tuple-element.529), channel_id=1, source_target_pairs={{64,0},{128,64},{192,128},{65,1},{129,65},{193,129},{66,2},{130,66... | collective-permute-start | bytes 1179656 | tf_op jit(solution)/shard_map/ppermute | solution.py:15
  19.2 0.8 copy-start.5
  23.5 5.7 copy-start.3
  33.1 1.6 copy-start.10
  33.1 1.6 copy-start.11
  282.5 2.3 copy-start.7
  284.7 425.0 %reduce-scatter.4.cloned.1.call-start = ((), (), s32[]{:S(2)}) async-start(), calls=%async_computation.6 | async-start | bytes 4259840
  293.4 9.4 %copy-start.9 = (f32[1,32,512]{2,1,0:T(8,128)S(1)}, f32[1,32,512]{2,1,0:T(8,128)}, u32[]{:S(2)}) copy-start(f32[1,32,512]{2,1,0:T(8,128)} %param.23) | copy-start | bytes 196612
  293.4 9.5 %copy-start.4 = (f32[2,256,256]{2,1,0:T(8,128)S(1)}, f32[2,256,256]{2,1,0:T(8,128)}, u32[]{:S(2)}) copy-start(f32[2,256,256]{2,1,0:T(8,128)} %param.18) | copy-start | bytes 1572868
  295.4 13.2 %collective-permute-start.2 = (f32[2,384,128]{1,2,0:T(8,128)}, f32[2,384,128]{1,2,0:T(8,128)}, u32[]{:S(2)}, u32[]{:S(2)}) collective-permute-start(f32[2,384,128]{1,2,0:T(8,128)} %get-tuple-element.527), channel_id=1, source_target_pairs={{0,64},{64,128},{128,192},{1,65},{65,129},{129,193},{2,66},{66,130... | collective-permute-start | bytes 1179656 | tf_op jit(solution)/shard_map/ppermute | solution.py:15
  301.5 11.5 %collective-permute-start.3 = (f32[2,384,128]{1,2,0:T(8,128)S(1)}, f32[2,384,128]{1,2,0:T(8,128)}, u32[]{:S(2)}, u32[]{:S(2)}) collective-permute-start(f32[2,384,128]{1,2,0:T(8,128)S(1)} %get-tuple-element.526), channel_id=1, source_target_pairs={{64,0},{128,64},{192,128},{65,1},{129,65},{193,129},{66,2},{130,66... | collective-permute-start | bytes 1179656 | tf_op jit(solution)/shard_map/ppermute | solution.py:15
  304.2 9.8 %copy-start.1 = (f32[1,2,384,512]{2,3,1,0:T(8,128)S(1)}, f32[1,2,384,512]{2,3,1,0:T(8,128)}, u32[]{:S(2)}) copy-start(f32[1,2,384,512]{2,3,1,0:T(8,128)} %copy.17) | copy-start | bytes 4718596
  314.2 1.1 copy-start.2
  318.4 156.0 %all-to-all-start = ((f32[16,1,1024]{2,1,0:T(1,128)}), f32[16,1,1024]{2,1,0:T(1,128)S(1)}, u32[]{:S(2)}, u32[]{:S(2)}) async-start(f32[16,1,1024]{2,1,0:T(1,128)} %reshape.139), calls=%async_computation | async-start | bytes 131072 | tf_op jit(solution)/shard_map/all_to_all | solution.py:145
  331.4 383.2 %all-reduce.6.cloned.1.call-start = ((), (), s32[]{:S(2)}) async-start(), calls=%async_computation.4 | async-start | bytes 1056768 | tf_op jit(solution)/shard_map/psum | solution.py:134
  474.3 324.0 %all-gather.2.cloned.1.call-start = ((), (), s32[]{:S(2)}) async-start(), calls=%async_computation.5 | async-start | bytes 2129920 | tf_op jit(solution)/shard_map/all_gather | solution.py:182
  803.7 4.0 copy-start.6
Sparse Core Ops, SparseCore 0:
  284.8 189.4 all-reduce.3
  476.6 47.1 all-reduce.5
Sparse Core Ops, SparseCore 1:
  293.5 416.2 reduce-scatter.3
  713.1 85.2 all-gather.1
